TPU v7x, 512 devices: a whole 4x8x8 slice. The times are simulated.
512 devices in a mesh: group: 64 (over y_lo, z, core), tp: 8 (over y_hi, x).
Axes of the slice: x: 4, y: 8 (y_hi: 2, y_lo: 4; y = y_hi * 4 + y_lo), z: 8, core: 2. Of those that a mesh axis runs over, the one named last changes fastest.
Arguments:
- tokens: bfloat16 [16384, 1024], P(('group', 'tp')), may hold values from -6 to 6
- variate: int32 [16384], P('group'), may hold values from 0 to 3
- time_ids: int32 [16384], P('group'), may hold values from 0 to 63
- cache_var: int32 [32768], P('group'), may hold values from 0 to 3
- cache_len: int32 [64], P('group'), may hold values from 1 to 512, as said below
- linked: int32 [64], P('group'), may hold values from 0 to 1, as said below
- cache_kv: bfloat16 [2, 32768, 1024], P(None, 'group', 'tp'), as said below
- var_bias: float32 [2, 16], P(None, 'tp'), may hold values from -2 to 2
- w_qkv: bfloat16 [3, 1024, 1024], P(None, None, 'tp'), may hold values from -0.1875 to 0.1875
- w_out: bfloat16 [1024, 1024], P('tp'), may hold values from -0.75 to 0.75
- w_gate_up: bfloat16 [2, 1024, 4096], P(None, None, 'tp'), may hold values from -0.1875 to 0.1875
- w_down: bfloat16 [4096, 1024], P('tp'), may hold values from -0.09375 to 0.09375
Outputs:
- layer_out: bfloat16 [16384, 1024], P(('group', 'tp'))
Inputs may be any that keep to these rules, and one draw needn't show every extreme that they name: Group g's cached prefix fills its first cache_len[g] slots; some group has all 512. linked[g] equals linked[g + 32]; groups 0 and 32 are linked, and some other pair is not. `cache_kv`: cached keys already rotated, and cached values.
All inputs are finite; a program needn't handle non-finite values.
Results may differ from a plain program's by a relative error of at most 0.023.
Values may be sent and summed in bfloat16 or wider, within the bound.
A program may use at most 64 MiB of HBM per device.

v0:
```python
import jax
import jax.numpy as jnp
from jax import lax
from jax.sharding import PartitionSpec as P

KEY_BLOCK = 128


far_future = 1073741824
masked_score = -1e30


def from_partner(block, axis, distance):
    count = lax.axis_size(axis)
    route = []
    for low in range(count):
        high = low | 1 << distance
        if high != low and high < count:
            route += [(low, high), (high, low)]
    return lax.ppermute(block, axis, route)


def normed(row_block):
    values = row_block.astype(jnp.float32)
    return values * lax.rsqrt(jnp.mean(values * values, axis=-1, keepdims=True) + 1e-05)


def rotary(values, position, head_count):
    row_count = values.shape[0]
    shaped = values.reshape(row_count, head_count, -1)
    half_width = shaped.shape[-1] // 2
    frequency = 10000.0 ** (-jnp.arange(half_width, dtype=jnp.float32) / half_width)
    angles = position.astype(jnp.float32)[:, None] * frequency[None, :]
    cosine = jnp.cos(angles)[:, None, :]
    sine_part = jnp.sin(angles)[:, None, :]
    lower_half = shaped[..., :half_width]
    upper_half = shaped[..., half_width:]
    turned = jnp.concatenate(
        [
            lower_half * cosine - upper_half * sine_part,
            upper_half * cosine + lower_half * sine_part,
        ],
        axis=-1,
    )
    return turned.reshape(row_count, -1)


def empty_partial(head_count, row_count, width):
    return (
        jnp.full((head_count, row_count), masked_score, jnp.float32),
        jnp.zeros((head_count, row_count), jnp.float32),
        jnp.zeros((head_count, row_count, width), jnp.float32),
    )


def attend(
    running,
    queries,
    query_time,
    query_var,
    key_vals,
    key_time,
    key_var,
    bias,
    first_block,
    block_count,
):
    head_count = bias.shape[1]
    query_heads = queries.reshape(queries.shape[0], head_count, -1)

    def one_block(block_index, carried):
        row_best, total, weighted = carried
        key_start = (first_block + block_index) * KEY_BLOCK
        block_kv = lax.dynamic_slice_in_dim(key_vals, key_start, KEY_BLOCK, 1)
        block_time = lax.dynamic_slice_in_dim(key_time, key_start, KEY_BLOCK, 0)
        block_var = lax.dynamic_slice_in_dim(key_var, key_start, KEY_BLOCK, 0)
        key_heads = block_kv[0].reshape(KEY_BLOCK, head_count, -1)
        value_heads = block_kv[1].reshape(KEY_BLOCK, head_count, -1)
        scores = (
            jnp.einsum("thd,khd->htk", query_heads, key_heads, preferred_element_type=jnp.float32)
            * 0.125
        )
        same_variate = (query_var[:, None] == block_var[None, :])[None]
        scores = scores + jnp.where(same_variate, bias[0][:, None, None], bias[1][:, None, None])
        visible = (block_time[None, :] <= query_time[:, None])[None]
        scores = jnp.where(visible, scores, masked_score)
        newest = jnp.maximum(row_best, jnp.max(scores, axis=-1))
        factor = jnp.exp(row_best - newest)
        weights = jnp.exp(scores - newest[..., None])
        total = total * factor + jnp.sum(weights, axis=-1)
        weighted = weighted * factor[..., None] + jnp.einsum(
            "htk,khd->htd",
            weights.astype(jnp.bfloat16),
            value_heads,
            preferred_element_type=jnp.float32,
        )
        return (newest, total, weighted)

    return lax.fori_loop(0, block_count, one_block, running)


def shards(
    tokens,
    variate,
    time_ids,
    cache_var,
    cache_len,
    linked,
    cache_kv,
    var_bias,
    w_qkv,
    w_out,
    w_gate_up,
    w_down,
):
    head_count = var_bias.shape[1]
    cache_rows = cache_kv.shape[1]
    local_rows = tokens.shape[0]
    all_rows = lax.all_gather(tokens, "tp", axis=0, tiled=True)
    group_rows = all_rows.shape[0]
    normal_in = normed(all_rows).astype(jnp.bfloat16)
    projected = jnp.einsum("td,cde->cte", normal_in, w_qkv, preferred_element_type=jnp.float32)
    queries = rotary(projected[0], time_ids, head_count).astype(jnp.bfloat16)
    new_keys = rotary(projected[1], time_ids, head_count).astype(jnp.bfloat16)
    new_vals = projected[2].astype(jnp.bfloat16)
    head_width = new_keys.shape[1] // head_count
    own_kv = jnp.concatenate([cache_kv, jnp.stack([new_keys, new_vals])], axis=1)
    length = cache_len[0]
    linked_flag = linked[0]
    slot_ids = jnp.arange(cache_rows, dtype=jnp.int32)
    own_time = jnp.concatenate(
        [jnp.where(slot_ids < length, -1, far_future).astype(jnp.int32), time_ids]
    )
    own_var = jnp.concatenate([cache_var, variate])
    cache_blocks = cache_rows // KEY_BLOCK
    new_blocks = group_rows // KEY_BLOCK
    partner_bit = lax.axis_size("group").bit_length() - 2
    running = empty_partial(head_count, group_rows, head_width)
    running = attend(
        running, queries, time_ids, variate, own_kv, own_time, own_var, var_bias, 0, cache_blocks
    )
    running = attend(
        running,
        queries,
        time_ids,
        variate,
        own_kv,
        own_time,
        own_var,
        var_bias,
        cache_blocks,
        new_blocks,
    )
    far_kv, far_time, far_var, far_len = from_partner(
        (own_kv, own_time, own_var, cache_len), "group", partner_bit
    )
    far_time = jnp.where(linked_flag > 0, far_time, far_future).astype(jnp.int32)
    running = attend(
        running, queries, time_ids, variate, far_kv, far_time, far_var, var_bias, 0, cache_blocks
    )
    running = attend(
        running,
        queries,
        time_ids,
        variate,
        far_kv,
        far_time,
        far_var,
        var_bias,
        cache_blocks,
        new_blocks,
    )
    row_best, total, weighted = running
    attn_heads = (
        (weighted / total[..., None])
        .transpose(1, 0, 2)
        .reshape(group_rows, -1)
        .astype(jnp.bfloat16)
    )
    attended = lax.psum(
        jnp.dot(attn_heads, w_out, preferred_element_type=jnp.float32).astype(jnp.bfloat16), "tp"
    ).astype(jnp.float32)
    stream = (all_rows.astype(jnp.float32) + attended).astype(jnp.bfloat16)
    normed_mid = normed(stream).astype(jnp.bfloat16)
    gate_up = jnp.einsum("td,cdf->ctf", normed_mid, w_gate_up, preferred_element_type=jnp.float32)
    hidden = (jax.nn.silu(gate_up[0]) * gate_up[1]).astype(jnp.bfloat16)
    ffn_out = lax.psum(
        jnp.dot(hidden, w_down, preferred_element_type=jnp.float32).astype(jnp.bfloat16), "tp"
    ).astype(jnp.float32)
    row_start = lax.axis_index("tp") * local_rows
    own_stream = lax.dynamic_slice_in_dim(stream, row_start, local_rows, 0)
    own_ffn = lax.dynamic_slice_in_dim(ffn_out, row_start, local_rows, 0)
    return (own_stream.astype(jnp.float32) + own_ffn).astype(jnp.bfloat16)


def solution(mesh):
    return jax.shard_map(
        shards,
        mesh=mesh,
        in_specs=(
            P(("group", "tp"), None),
            P("group"),
            P("group"),
            P("group"),
            P("group"),
            P("group"),
            P(None, "group", "tp"),
            P(None, "tp"),
            P(None, None, "tp"),
            P("tp", None),
            P(None, None, "tp"),
            P("tp", None),
        ),
        out_specs=P(("group", "tp"), None),
        check_vma=False,
    )
```

profile of v0, /device:TPU:64, one launch (start us, length us, event | category | flops | bytes accessed | tf_op | source)
XLA Modules:
  0.0 345.2 jit_solution(3147307985806670945)
XLA Ops:
  6.6 46.0 %all_gather.3 = bf16[256,1024]{1,0:T(8,128)(2,1)S(1)} all-gather(bf16[32,1024]{1,0:T(8,128)(2,1)} %param.20), channel_id=1, replica_groups=mesh['group'=64,'tp'=8] {'tp'}, dimensions={0}, use_global_device_ids=true | all-gather | bytes 589824 | tf_op jit(solution)/shard_map/all_gather | solution.py:119
  52.7 1.4 copy.17
  54.7 1.1 copy.18
  56.9 3.4 collective-permute-start.1
  60.3 1.3 constant_dynamic-update-slice_fusion.1
  61.6 1.3 constant_dynamic-update-slice_fusion
  62.9 3.3 collective-permute-start.2
  67.4 3.4 collective-permute-start
  71.5 15.4 %while.72 = (s32[]{:T(128)}, f32[2,256]{1,0:T(2,128)S(1)}, f32[2,256]{1,0:T(2,128)S(1)}, f32[2,256,64]{1,2,0:T(8,128)S(1)}, s32[768]{0:T(1024)}, /*index=5*/s32[...) while((s32[]{:T(128)}, f32[2,256]{1,0:T(2,128)S(1)}, ...), condition=%wide.region_4.5_spmd.clone, body=%wide.region_1.4_spmd.clone.sunk | while | flops 17533448 | bytes 1479963 | solution.py:99
  73.1 0.8 constant_dynamic-slice_fusion.15
  73.9 1.1 fusion.118
  77.0 0.8 constant_dynamic-slice_fusion.15
  77.8 1.1 fusion.118
  81.6 1.1 fusion.118
  85.5 1.1 fusion.118
  86.9 7.7 %while.69 = (s32[]{:T(128)}, f32[2,256]{1,0:T(2,128)S(1)}, f32[2,256]{1,0:T(2,128)S(1)}, f32[2,256,64]{1,2,0:T(8,128)S(1)}, s32[768]{0:T(1024)}, /*index=5*/s32[...) while((s32[]{:T(128)}, f32[2,256]{1,0:T(2,128)S(1)}, ...), condition=%wide.region_8.9_spmd, body=%wide.region_5.8_spmd.sunk | while | flops 17499144 | bytes 1479971 | solution.py:99
  89.3 1.1 fusion.100
  93.2 1.1 fusion.100
  95.3 6.9 %while.70 = (s32[]{:T(128)}, f32[2,256]{1,0:T(2,128)S(1)}, f32[2,256]{1,0:T(2,128)S(1)}, f32[2,256,64]{1,2,0:T(8,128)S(1)}, s32[768]{0:T(1024)S(1)}, /*index=5*/...) while((s32[]{:T(128)}, f32[2,256]{1,0:T(2,128)S(1)}, ...), condition=%wide.region_12.13_spmd, body=%wide.region_9.12_spmd.sunk | while | flops 17499144 | bytes 1479951 | solution.py:99
  95.6 1.1 fusion.106
  97.4 1.1 fusion.106
  99.1 1.1 fusion.106
  100.8 1.1 fusion.106
  102.3 3.5 %while.71 = (s32[]{:T(128)}, f32[2,256]{1,0:T(2,128)S(1)}, f32[2,256]{1,0:T(2,128)S(1)}, f32[2,256,64]{1,2,0:T(8,128)S(1)}, s32[768]{0:T(1024)S(1)}, /*index=5*/...) while((s32[]{:T(128)}, f32[2,256]{1,0:T(2,128)S(1)}, ...), condition=%wide.region_16.17_spmd, body=%wide.region_13.16_spmd.sunk | while | flops 17499144 | bytes 1479971 | solution.py:99
  102.6 1.1 fusion.112
  104.3 1.1 fusion.112
  105.8 1.1 convolution_convert_fusion.1
  107.0 116.5 %all-reduce.3.cloned.1.call-done = bf16[256,1024]{1,0:T(8,128)(2,1)} async-done(((bf16[256,1024]{1,0:T(8,128)(2,1)}), bf16[256,1024]{1,0:T(8,128)(2,1)}) %all-reduce.3.cloned.1.call-update) | async-done | bytes 524304 | tf_op jit(solution)/shard_map/psum | solution.py:180
  223.5 1.3 fusion.30
  226.0 1.3 convolution_convert_fusion
  227.3 109.5 %all-reduce.5.cloned.1.call-done = bf16[256,1024]{1,0:T(8,128)(2,1)} async-done(((bf16[256,1024]{1,0:T(8,128)(2,1)}), bf16[256,1024]{1,0:T(8,128)(2,1)}) %all-reduce.5.cloned.1.call-update) | async-done | bytes 524304 | tf_op jit(solution)/shard_map/psum | solution.py:187
  336.8 1.5 add_convert_fusion
  (161 shorter events, 22.2 us)
Async XLA Ops:
  6.5 218.3 %copy-start = (bf16[2,1024,512]{2,1,0:T(8,128)(2,1)S(1)}, bf16[2,1024,512]{2,1,0:T(8,128)(2,1)}, u32[]{:S(2)}) copy-start(bf16[2,1024,512]{2,1,0:T(8,128)(2,1)} %param.30) | copy-start | bytes 6291460
  6.5 217.0 %all-reduce.3.cloned.1.call-start = ((), (), s32[]{:S(2)}) async-start(), calls=%async_computation | async-start | bytes 1048576 | tf_op jit(solution)/shard_map/psum | solution.py:180
  52.7 2.0 copy-start.1
  54.1 6.2 %copy-start.5 = (s32[512]{0:T(512)S(1)}, s32[512]{0:T(512)}, u32[]{:S(2)}) copy-start(s32[512]{0:T(512)} %param.23) | copy-start | bytes 6148
  54.1 7.5 %copy-start.2 = (s32[256]{0:T(256)S(1)}, s32[256]{0:T(256)}, u32[]{:S(2)}) copy-start(s32[256]{0:T(256)} %param.21) | copy-start | bytes 3076
  54.1 17.4 %copy-start.3 = (f32[2,2]{1,0:T(2,128)S(1)}, f32[2,2]{1,0:T(2,128)}, u32[]{:S(2)}) copy-start(f32[2,2]{1,0:T(2,128)} %param.27) | copy-start | bytes 52
  56.9 38.4 %collective-permute-start.1 = (bf16[2,768,128]{1,2,0:T(8,128)(2,1)}, bf16[2,768,128]{1,2,0:T(8,128)(2,1)S(1)}, u32[]{:S(2)}, u32[]{:S(2)}) collective-permute-start(bf16[2,768,128]{1,2,0:T(8,128)(2,1)} %maximum_maximum_fusion), channel_id=1, source_target_pairs={{0,256},{256,0},{8,264},{264,8},{16,272},{272,16},{24,280},{280,24... | collective-permute-start | bytes 1179656 | tf_op jit(solution)/shard_map/ppermute | solution.py:20
  62.9 32.4 %collective-permute-start.2 = (s32[768]{0:T(1024)}, s32[768]{0:T(1024)S(1)}, u32[]{:S(2)}, u32[]{:S(2)}) collective-permute-start(s32[768]{0:T(1024)} %constant_dynamic-update-slice_fusion), channel_id=1, source_target_pairs={{0,256},{256,0},{8,264},{264,8},{16,272},{272,16},{24,280},{280,24... | collective-permute-start | bytes 9224 | tf_op jit(solution)/shard_map/ppermute | solution.py:20
  67.4 27.9 %collective-permute-start = (s32[768]{0:T(1024)}, s32[768]{0:T(1024)S(1)}, u32[]{:S(2)}, u32[]{:S(2)}) collective-permute-start(s32[768]{0:T(1024)} %pad_add_fusion), channel_id=1, source_target_pairs={{0,256},{256,0},{8,264},{264,8},{16,272},{272,16},{24,280},{280,24... | collective-permute-start | bytes 9224 | tf_op jit(solution)/shard_map/ppermute | solution.py:20
  102.3 3.5 %copy-start.4 = (bf16[128,1024]{1,0:T(8,128)(2,1)S(1)}, bf16[128,1024]{1,0:T(8,128)(2,1)}, u32[]{:S(2)}) copy-start(bf16[128,1024]{1,0:T(8,128)(2,1)} %param.29) | copy-start | bytes 786436
  106.9 229.9 %all-reduce.5.cloned.1.call-start = ((), (), s32[]{:S(2)}) async-start(), calls=%async_computation.1 | async-start | bytes 1048576 | tf_op jit(solution)/shard_map/psum | solution.py:187
  224.8 1.2 copy-start.6
Sparse Core Ops, SparseCore 0:
  107.1 116.3 all-reduce.2
  227.5 109.3 all-reduce.4
where the time goes:
time: 347 us; the launch traced here: 345 us
  waiting for transfers between devices  226 us (65%)
  blocking collectives  46 us (13%)
  local copies, waits for them, and re-layouts  20.4 us (6%)
  matrix products  19.2 us (6%)
  between operations  15 us (4%)
  starting transfers between devices  10.2 us (3%)
  other arithmetic  7.54 us (2%)
    psum x1, waiting for transfers between devices, shards(): lax.psum(jnp.dot(attn_heads, w_out, preferred_element_type=jnp.float32).a...  117 us
    psum x1, waiting for transfers between devices, shards(): lax.psum(jnp.dot(hidden, w_down, preferred_element_type=jnp.float32).asty...  109 us
    all_gather x1, blocking collectives, shards(): all_rows = lax.all_gather(tokens, 'tp', axis=0, tiled=True)  46 us
    dot_general x12, matrix products, one_block(): jnp.einsum('thd,khd->htk', query_heads, key_heads, preferred_element_type...  13.2 us
    ppermute x3, starting transfers between devices, from_partner(): return lax.ppermute(block, axis, route)  10.2 us
  transfers between devices with their start and end apart: 5, of which 2 were waited for; matrix products, arithmetic and copies ran while one was open for 8% of the time, Pallas kernels for 0%

commit v1 on v0

v1 whole, which is shorter than its diff:
```python
import jax
import jax.numpy as jnp
from jax import lax
from jax.experimental import pallas as pl
from jax.experimental.pallas import tpu as pltpu
from jax.sharding import PartitionSpec as P

F32 = jnp.float32
BF16 = jnp.bfloat16
MASKED = -1e30
GROUPS = 64
TP = 8
XN = 4
ROWS = 32
TOK = 256
HALF = 128
CACHE = 512
KEYS = CACHE + TOK
D = 1024
HW = 128
HD = 64
FF = 512

TY, TX, TF, ME, QQ, O1, O2, AX, W1, W2, W3, W4, RF, RN, RY, NSEM = (
    0, 1, 4, 7, 8, 9, 11, 15, 18, 19, 22, 25, 29, 32, 35, 36,
)


def dot(a, b):
    return jnp.dot(a, b, preferred_element_type=F32)


def normed(values):
    return values * lax.rsqrt(jnp.mean(values * values, axis=-1, keepdims=True) + 1e-05)


def spread(row):
    return jnp.broadcast_to(row, (HW, row.shape[1])).T


def layer(
    tok, tim, var, cvar, clen, lnk, ckv, vb, wqkv, wo, wgu, wd,
    out,
    x_all, wq, ke, vn, vt, qs, qe, qr, qe2, me_s, me_r, cvr, cs, sn,
    o1s, s1s, o1r, s1r, o2s, s2s, o2r, s2r,
    a3, wof, wguv, wdv, st, hid, far, near, rf, rn, ys, yr,
    ssem, rsem, lsem,
):
    g = lax.axis_index("group")
    t = lax.axis_index("tp")
    x = lax.rem(t, XN)
    yh = lax.div(t, XN)
    core = lax.rem(g, 2)
    t_far = lax.rem(t + XN, TP)
    g_par = lax.rem(g + GROUPS // 2, GROUPS)
    g_sib = g + 1 - 2 * core

    def xpeer(k):
        return (g, yh * XN + lax.rem(x + k, XN))

    ypeer = (g, t_far)
    ppeer = (g_par, t)
    fpeer = (g_par, t_far)
    speer = (g_sib, t)

    def remote(slot, src, dst, peer):
        return pltpu.make_async_remote_copy(
            src_ref=src, dst_ref=dst, send_sem=ssem.at[slot], recv_sem=rsem.at[slot],
            device_id=peer, device_id_type=pl.DeviceIdType.MESH,
        )

    barrier = pltpu.get_barrier_semaphore()
    for peer in (ypeer, ppeer, fpeer, speer, xpeer(1), xpeer(2), xpeer(3)):
        pl.semaphore_signal(barrier, inc=1, device_id=peer, device_id_type=pl.DeviceIdType.MESH)

    own_rows = pl.ds(pl.multiple_of(t * ROWS, ROWS), ROWS)
    far_rows = pl.ds(pl.multiple_of(t_far * ROWS, ROWS), ROWS)

    def local(slot, src, dst):
        copy = pltpu.make_async_copy(src, dst, lsem.at[slot])
        copy.start()
        return copy

    ld_tok = local(0, tok, x_all.at[own_rows])
    ld_tim = local(1, tim, me_s.at[pl.ds(0, 1)])
    ld_var = local(2, var, me_s.at[pl.ds(1, 1)])
    ld_cvar = local(3, cvar, cvr)
    ld_w = [local(4 + c, wqkv.at[c], wq.at[:, pl.ds(c * HW, HW)]) for c in range(3)]
    ld_k = local(7, ckv.at[0], ke.at[pl.ds(0, CACHE), pl.ds(0, HW)])
    ld_v = local(8, ckv.at[1], vn)
    ld_wo = [local(9 + c, wo.at[pl.ds(c * HD, HD)], wof.at[x, yh, c]) for c in range(2)]
    ld_gu = [local(11 + c, wgu.at[c], wguv.at[:, pl.ds(c * FF, FF)]) for c in range(2)]
    ld_d = local(13, wd, wdv)
    ld_tok.wait()
    ld_tim.wait()
    ld_var.wait()
    pl.semaphore_wait(barrier, 7)

    tok_y = remote(TY, x_all.at[own_rows], x_all.at[own_rows], ypeer)
    tok_y.start()
    tok_x = [remote(TX + k, x_all.at[own_rows], x_all.at[own_rows], xpeer(k + 1)) for k in range(3)]
    for copy in tok_x:
        copy.start()
    meta = remote(ME, me_s, me_r, ppeer)
    meta.start()

    time_row = me_s[0:1, :].astype(F32)
    var_row = me_s[1:2, :].astype(F32)
    freq = jnp.exp(
        lax.broadcasted_iota(jnp.int32, (HD // 2, TOK), 0).astype(F32) * (-9.210340371976184 / 32)
    )
    angle = freq * time_row
    cs[...] = jnp.cos(angle)
    sn[...] = jnp.sin(angle)

    lane = lax.broadcasted_iota(jnp.int32, (CACHE, HW), 1)
    slot = lax.broadcasted_iota(jnp.int32, (CACHE, HW), 0)
    lane_var = lax.rem(lane, 4).astype(F32)
    in_var = (lane >= HD) & (lane < HD + 12)
    ld_cvar.wait()
    same = jnp.where(spread(cvr[...].astype(F32)) == lane_var, 1.0, 0.0)
    shut = jnp.where(slot >= clen[0], MASKED, 0.0)
    ke[0:CACHE, HW:] = jnp.where(lane < HD, shut, jnp.where(in_var, same, 0.0)).astype(BF16)
    lane = lane[:TOK]
    same = jnp.where(spread(var_row) == lane_var[:TOK], 1.0, 0.0)
    shut = jnp.where(spread(time_row) > lane.astype(F32), MASKED, 0.0)
    ke[CACHE:, HW:] = jnp.where(lane < HD, shut, jnp.where(in_var[:TOK], same, 0.0)).astype(BF16)

    def query_side(dst, times, variates):
        row = lax.broadcasted_iota(jnp.int32, (HD, TOK), 0)
        at_time = jnp.where(row.astype(F32) == times, 1.0, 0.0).astype(BF16)
        hit = lax.rem(row, 4).astype(F32) == variates
        for h in range(2):
            bias = jnp.where(hit, vb[0, h], vb[1, h])
            high = bias.astype(BF16).astype(F32)
            mid = (bias - high).astype(BF16).astype(F32)
            low = bias - high - mid
            parts = jnp.where(
                row < 4, high, jnp.where(row < 8, mid, jnp.where(row < 12, low, 0.0))
            )
            dst[h, HW : HW + HD, :] = at_time
            dst[h, HW + HD :, :] = parts.astype(BF16)
            dst[h, (1 - h) * HD : (2 - h) * HD, :] = jnp.zeros((HD, TOK), BF16)

    query_side(qe, time_row, var_row)
    ld_v.wait()
    vt[:, 0:CACHE] = vn[...].astype(F32).T.astype(BF16)
    for copy in ld_w:
        copy.wait()
    for copy in ld_wo:
        copy.wait()

    tok_y.wait_send()
    w1 = remote(W1, wof.at[x, yh, core], wof.at[x, yh, core], ypeer)
    w1.start()

    def qkv(half):
        base = pl.multiple_of(half * HALF, HALF)
        rows = pl.ds(base, HALF)
        normal = normed(x_all[rows, :].astype(F32)).astype(BF16)
        prod = dot(normal, wq[...])
        cosine = cs[:, rows]
        sine = sn[:, rows]

        def turned(u):
            parts = []
            for h in range(2):
                lo = u[h * HD : h * HD + HD // 2]
                hi = u[h * HD + HD // 2 : (h + 1) * HD]
                parts += [lo * cosine - hi * sine, hi * cosine + lo * sine]
            return jnp.concatenate(parts, axis=0)

        q = turned(prod[:, 0:HW].T).astype(BF16).astype(F32) * 0.125
        qs[:, rows] = q.astype(BF16)
        k = turned(prod[:, HW : 2 * HW].T)
        v = prod[:, 2 * HW :].T
        new = pl.ds(pl.multiple_of(base + CACHE, HALF), HALF)
        return (new, k, v)

    def keep(new, k, v):
        ke[new, 0:HW] = k.T.astype(BF16)
        vt[:, new] = v.astype(BF16)

    tok_y.wait_recv()
    tok_f = [remote(TF + k, x_all.at[far_rows], x_all.at[far_rows], xpeer(k + 1)) for k in range(3)]
    for copy in tok_f:
        copy.start()
    for copy in tok_x:
        copy.wait_recv()
    keep(*qkv(yh))
    w2 = [remote(W2 + k, wof.at[x, yh, core], wof.at[x, yh, core], xpeer(k + 1)) for k in range(3)]
    for copy in w2:
        copy.start()
    for copy in tok_f:
        copy.wait_recv()
    rest = qkv(1 - yh)
    send_q = remote(QQ, qs, qr, ppeer)
    send_q.start()
    keep(*rest)
    ld_k.wait()

    def attend(dst, h):
        s = dot(ke[...], dst[h])
        best = jnp.max(s, axis=0, keepdims=True)
        p = jnp.exp(s - best)
        total = jnp.sum(p, axis=0, keepdims=True)
        o = dot(vt[h * HD : (h + 1) * HD, :], p.astype(BF16))
        return o, best, total

    def both_heads(dst, q, o_ref, s_ref):
        s_ref[...] = jnp.zeros(s_ref.shape, F32)
        for h in range(2):
            dst[h, h * HD : (h + 1) * HD, :] = q[h * HD : (h + 1) * HD, :]
            o, best, total = attend(dst, h)
            o_ref[h * HD : (h + 1) * HD, :] = o.astype(BF16)
            s_ref[h : h + 1, :] = best
            s_ref[2 + h : 3 + h, :] = total

    both_heads(qe, qs, o1s, s1s)
    send_o1 = [remote(O1, o1s, o1r, ypeer), remote(O1 + 1, s1s, s1r, ypeer)]
    for copy in send_o1:
        copy.start()

    meta.wait_recv()
    query_side(qe2, me_r[0:1, :].astype(F32), me_r[1:2, :].astype(F32))
    send_q.wait_recv()
    both_heads(qe2, qr, o2s, s2s)
    send_o2 = [
        remote(O2, o2s, o2r.at[0], ppeer), remote(O2 + 1, s2s, s2r.at[0], ppeer),
        remote(O2 + 2, o2s, o2r.at[1], fpeer), remote(O2 + 3, s2s, s2r.at[1], fpeer),
    ]
    for copy in send_o2:
        copy.start()

    yf = 1 - yh
    w1.wait_recv()
    w3 = [remote(W3 + k, wof.at[x, yf, core], wof.at[x, yf, core], xpeer(k + 1)) for k in range(3)]
    for copy in w3:
        copy.start()
    w4 = [remote(W4, wof.at[x, yf, core], wof.at[x, yf, core], speer)]
    w4[0].start()

    def merged(o_a, s_a, o_b, s_b):
        on = lnk[0] > 0
        parts = []
        for h in range(2):
            head = slice(h * HD, (h + 1) * HD)
            m_a = s_a[h : h + 1, :]
            m_b = jnp.where(on, s_b[h : h + 1, :], MASKED)
            best = jnp.maximum(m_a, m_b)
            f_a = jnp.exp(m_a - best)
            f_b = jnp.where(on, jnp.exp(m_b - best), 0.0)
            total = f_a * s_a[2 + h : 3 + h, :] + f_b * s_b[2 + h : 3 + h, :]
            parts.append(
                (f_a * o_a[head, :].astype(F32) + f_b * o_b[head, :].astype(F32)) / total
            )
        return jnp.concatenate(parts, axis=0).T

    for copy in send_o1:
        copy.wait_recv()
    for copy in send_o2:
        copy.wait_recv()
    mine = merged(o1s, s1s, o2r.at[0], s2r.at[0])
    other = merged(o1r, s1r, o2r.at[1], s2r.at[1])
    a3[x, :, 0:HW] = jnp.where(yh == 0, mine, other).astype(BF16)
    a3[x, :, HW:] = jnp.where(yh == 0, other, mine).astype(BF16)
    send_a = [remote(AX + k, a3.at[x], a3.at[x], xpeer(k + 1)) for k in range(3)]
    for copy in send_a:
        copy.start()

    for k in range(3):
        w2[k].wait_recv()
        w3[k].wait_recv()
        xk = lax.rem(x + 3 - k, XN)
        copy = remote(W4 + 1 + k, wof.at[xk, :, core], wof.at[xk, :, core], speer)
        copy.start()
        w4.append(copy)

    for copy in w4:
        copy.wait_recv()
    st[...] = x_all[...].astype(F32)
    st[...] += dot(a3[x], wof[x].reshape(2 * HW, D))
    for k in (0, 2, 1):
        send_a[k].wait_recv()
        xk = lax.rem(x + 3 - k, XN)
        st[...] += dot(a3[xk], wof[xk].reshape(2 * HW, D))

    for copy in ld_gu:
        copy.wait()
    ld_d.wait()
    for half in range(2):
        rows = slice(half * HALF, (half + 1) * HALF)
        stream = st[rows, :].astype(BF16).astype(F32)
        st[rows, :] = stream
        gate_up = dot(normed(stream).astype(BF16), wguv[...])
        gate = gate_up[:, :FF]
        hid[rows, :] = (gate / (1.0 + jnp.exp(-gate)) * gate_up[:, FF:]).astype(BF16)

    def down(half, dst):
        dst[...] = dot(hid[pl.ds(pl.multiple_of(half * HALF, HALF), HALF), :], wdv[...]).astype(BF16)

    def block(k):
        return pl.ds(pl.multiple_of(lax.rem(x + k, XN) * ROWS, ROWS), ROWS)

    down(yf, far)
    send_f = [remote(RF + k, far.at[block(k + 1)], rf.at[k], xpeer(k + 1)) for k in range(3)]
    for copy in send_f:
        copy.start()
    down(yh, near)
    send_n = [remote(RN + k, near.at[block(k + 1)], rn.at[k], xpeer(k + 1)) for k in range(3)]
    for copy in send_n:
        copy.start()
    total = far[block(0), :].astype(F32)
    for k in range(3):
        send_f[k].wait_recv()
        total = total + rf[k].astype(F32)
    ys[...] = total.astype(BF16)
    send_y = remote(RY, ys, yr, ypeer)
    send_y.start()
    total = near[block(0), :].astype(F32)
    for k in range(3):
        send_n[k].wait_recv()
        total = total + rn[k].astype(F32)
    total = total + st[own_rows, :]
    for copy in [tok_y][:0] + tok_x + tok_f + [meta, w1, send_q] + w2 + w3 + w4 + send_o1 + send_o2 + send_a:
        copy.wait_send()
    for copy in send_f + send_n:
        copy.wait_send()
    send_y.wait_recv()
    out[...] = (total + yr[...].astype(F32)).astype(BF16)
    send_y.wait_send()


def shards(
    tokens, variate, time_ids, cache_var, cache_len, linked, cache_kv, var_bias,
    w_qkv, w_out, w_gate_up, w_down,
):
    anyspace = pl.BlockSpec(memory_space=pl.ANY)
    smem = pl.BlockSpec(memory_space=pltpu.SMEM)
    vmem = pltpu.VMEM
    scratch = [
        vmem((TOK, D), BF16),
        vmem((D, 3 * HW), BF16),
        vmem((KEYS, 2 * HW), BF16),
        vmem((CACHE, HW), BF16),
        vmem((HW, KEYS), BF16),
        vmem((HW, TOK), BF16),
        vmem((2, 2 * HW, TOK), BF16),
        vmem((HW, TOK), BF16),
        vmem((2, 2 * HW, TOK), BF16),
        vmem((2, TOK), jnp.int32),
        vmem((2, TOK), jnp.int32),
        vmem((1, CACHE), jnp.int32),
        vmem((HD // 2, TOK), F32),
        vmem((HD // 2, TOK), F32),
        vmem((HW, TOK), BF16), vmem((8, TOK), F32),
        vmem((HW, TOK), BF16), vmem((8, TOK), F32),
        vmem((HW, TOK), BF16), vmem((8, TOK), F32),
        vmem((2, HW, TOK), BF16), vmem((2, 8, TOK), F32),
        vmem((XN, TOK, 2 * HW), BF16),
        vmem((XN, 2, 2, HD, D), BF16),
        vmem((D, 2 * FF), BF16),
        vmem((FF, D), BF16),
        vmem((TOK, D), F32),
        vmem((TOK, FF), BF16),
        vmem((HALF, D), BF16),
        vmem((HALF, D), BF16),
        vmem((3, ROWS, D), BF16),
        vmem((3, ROWS, D), BF16),
        vmem((ROWS, D), BF16),
        vmem((ROWS, D), BF16),
        pltpu.SemaphoreType.DMA((NSEM,)),
        pltpu.SemaphoreType.DMA((NSEM,)),
        pltpu.SemaphoreType.DMA((14,)),
    ]
    return pl.pallas_call(
        layer,
        out_shape=jax.ShapeDtypeStruct((ROWS, D), BF16),
        in_specs=[
            anyspace, anyspace, anyspace, anyspace, smem, smem, anyspace, smem,
            anyspace, anyspace, anyspace, anyspace,
        ],
        out_specs=pl.BlockSpec(memory_space=pltpu.VMEM),
        scratch_shapes=scratch,
        compiler_params=pltpu.CompilerParams(
            collective_id=0, has_side_effects=True, vmem_limit_bytes=48 << 20
        ),
        name="layer",
    )(
        tokens, time_ids.reshape(1, TOK), variate.reshape(1, TOK), cache_var.reshape(1, CACHE),
        cache_len, linked, cache_kv, var_bias, w_qkv, w_out, w_gate_up, w_down,
    )


def solution(mesh):
    return jax.shard_map(
        shards,
        mesh=mesh,
        in_specs=(
            P(("group", "tp"), None),
            P("group"),
            P("group"),
            P("group"),
            P("group"),
            P("group"),
            P(None, "group", "tp"),
            P(None, "tp"),
            P(None, None, "tp"),
            P("tp", None),
            P(None, None, "tp"),
            P("tp", None),
        ),
        out_specs=P(("group", "tp"), None),
        check_vma=False,
    )
```

time: 347 us -> 63.1 us (0.18)
  the two profiles are of different devices: /device:TPU:64 before, /device:TPU:12 now
where the time goes in v1:
time: 63.1 us; the launch traced here: 62.7 us
  Pallas kernels  51.3 us (81%)
  local copies, waits for them, and re-layouts  10 us (16%)
  between operations  1.32 us (2%)
    pallas_call x1, Pallas kernels, shards(): pl.pallas_call(layer, out_shape=jax.ShapeDtypeStruct((ROWS, D), BF16), in...  51.3 us
    unnamed x21, local copies, waits for them, and re-layouts  10 us

profile of v1, /device:TPU:12, one launch (start us, length us, event | category | flops | bytes accessed | tf_op | source)
XLA Modules:
  0.0 62.7 jit_solution(1090841498858786411)
XLA Ops:
  1.3 0.0 copy-start
  1.3 1.6 %copy-done = bf16[2,1024,512]{2,1,0:T(8,128)(2,1)S(1)} copy-done((bf16[2,1024,512]{2,1,0:T(8,128)(2,1)S(1)}, bf16[2,1024,512]{2,1,0:T(8,128)(2,1)}, u32[]{:S(2)}) %copy-start) | copy-done | bytes 2097176
  2.9 0.0 copy-start.1
  2.9 1.2 %copy-done.1 = bf16[512,1024]{1,0:T(8,128)(2,1)S(1)} copy-done((bf16[512,1024]{1,0:T(8,128)(2,1)S(1)}, bf16[512,1024]{1,0:T(8,128)(2,1)}, u32[]{:S(2)}) %copy-start.1) | copy-done | bytes 1048600
  4.1 0.0 copy-start.2
  4.1 1.1 %copy-done.2 = bf16[3,1024,128]{2,1,0:T(8,128)(2,1)S(1)} copy-done((bf16[3,1024,128]{2,1,0:T(8,128)(2,1)S(1)}, bf16[3,1024,128]{2,1,0:T(8,128)(2,1)}, u32[]{:S(2)}) %copy-start.2) | copy-done | bytes 786456
  5.2 0.0 copy-start.3
  5.3 0.9 %copy-done.3 = bf16[2,512,128]{2,1,0:T(8,128)(2,1)S(1)} copy-done((bf16[2,512,128]{2,1,0:T(8,128)(2,1)S(1)}, bf16[2,512,128]{2,1,0:T(8,128)(2,1)}, u32[]{:S(2)}) %copy-start.3) | copy-done | bytes 262168
  6.2 0.0 copy-start.4
  6.2 0.9 %copy-done.4 = bf16[128,1024]{1,0:T(8,128)(2,1)S(1)} copy-done((bf16[128,1024]{1,0:T(8,128)(2,1)S(1)}, bf16[128,1024]{1,0:T(8,128)(2,1)}, u32[]{:S(2)}) %copy-start.4) | copy-done | bytes 262168
  7.1 0.0 copy-start.5
  7.2 0.8 %copy-done.5 = bf16[32,1024]{1,0:T(8,128)(2,1)S(1)} copy-done((bf16[32,1024]{1,0:T(8,128)(2,1)S(1)}, bf16[32,1024]{1,0:T(8,128)(2,1)}, u32[]{:S(2)}) %copy-start.5) | copy-done | bytes 65560
  8.0 0.0 copy-start.6
  8.0 0.7 %copy-done.6 = s32[512]{0:T(512)S(1)} copy-done((s32[512]{0:T(512)S(1)}, s32[512]{0:T(512)}, u32[]{:S(2)}) %copy-start.6) | copy-done | bytes 2072
  8.7 0.0 copy-start.7
  8.7 0.7 %copy-done.7 = s32[256]{0:T(256)S(1)} copy-done((s32[256]{0:T(256)S(1)}, s32[256]{0:T(256)}, u32[]{:S(2)}) %copy-start.7) | copy-done | bytes 1048
  9.4 0.0 copy-start.8
  9.4 0.7 %copy-done.8 = s32[256]{0:T(256)S(1)} copy-done((s32[256]{0:T(256)S(1)}, s32[256]{0:T(256)}, u32[]{:S(2)}) %copy-start.8) | copy-done | bytes 1048
  10.0 0.0 copy-start.9
  10.0 0.7 %copy-done.9 = f32[2,2]{1,0:T(2,128)S(1)} copy-done((f32[2,2]{1,0:T(2,128)S(1)}, f32[2,2]{1,0:T(2,128)}, u32[]{:S(2)}) %copy-start.9) | copy-done | bytes 40
  10.7 51.3 %layer.1 = bf16[32,1024]{1,0:T(8,128)(2,1)S(1)} custom-call(bf16[32,1024]{1,0:T(8,128)(2,1)S(1)} %copy-done.5, s32[1,256]{1,0:T(1,128)S(1)} %bitcast.4, s32[1,256]{1,0:T(1,128)S(1)} %bitcast.5, s32[1,512]{1,0:T(1,128)S(1)} %bitcast.3, s32[1]{0:T(128)S(6)} %copy.14.clen, s32[1]{0:T(128)S(6)} %copy.15.lnk, bf16[2,512,128]{2,1,0:T(8,128)(2,1)S(1)} %copy-done.3, ...), custom_call_target="tpu_custom_call" | custom-call | tf_op jit(solution)/shard_map/layer/pallas_call | solution.py:376
  62.1 0.6 %copy.16 = bf16[32,1024]{1,0:T(8,128)(2,1)} copy(bf16[32,1024]{1,0:T(8,128)(2,1)S(1)} %layer.1) | data formatting | bytes 131072
Async XLA Ops:
  1.3 1.6 %copy-start = (bf16[2,1024,512]{2,1,0:T(8,128)(2,1)S(1)}, bf16[2,1024,512]{2,1,0:T(8,128)(2,1)}, u32[]{:S(2)}) copy-start(bf16[2,1024,512]{2,1,0:T(8,128)(2,1)} %wgu.1) | copy-start | bytes 6291460
  2.9 1.2 %copy-start.1 = (bf16[512,1024]{1,0:T(8,128)(2,1)S(1)}, bf16[512,1024]{1,0:T(8,128)(2,1)}, u32[]{:S(2)}) copy-start(bf16[512,1024]{1,0:T(8,128)(2,1)} %wd.1) | copy-start | bytes 3145732
  4.1 1.1 %copy-start.2 = (bf16[3,1024,128]{2,1,0:T(8,128)(2,1)S(1)}, bf16[3,1024,128]{2,1,0:T(8,128)(2,1)}, u32[]{:S(2)}) copy-start(bf16[3,1024,128]{2,1,0:T(8,128)(2,1)} %wqkv.1) | copy-start | bytes 2359300
  5.2 0.9 %copy-start.3 = (bf16[2,512,128]{2,1,0:T(8,128)(2,1)S(1)}, bf16[2,512,128]{2,1,0:T(8,128)(2,1)}, u32[]{:S(2)}) copy-start(bf16[2,512,128]{2,1,0:T(8,128)(2,1)} %ckv.1) | copy-start | bytes 786436
  6.2 0.9 %copy-start.4 = (bf16[128,1024]{1,0:T(8,128)(2,1)S(1)}, bf16[128,1024]{1,0:T(8,128)(2,1)}, u32[]{:S(2)}) copy-start(bf16[128,1024]{1,0:T(8,128)(2,1)} %wo.1) | copy-start | bytes 786436
  7.1 0.8 %copy-start.5 = (bf16[32,1024]{1,0:T(8,128)(2,1)S(1)}, bf16[32,1024]{1,0:T(8,128)(2,1)}, u32[]{:S(2)}) copy-start(bf16[32,1024]{1,0:T(8,128)(2,1)} %tok.1) | copy-start | bytes 196612
  8.0 0.7 %copy-start.6 = (s32[512]{0:T(512)S(1)}, s32[512]{0:T(512)}, u32[]{:S(2)}) copy-start(s32[512]{0:T(512)} %param.15) | copy-start | bytes 6148
  8.7 0.7 %copy-start.7 = (s32[256]{0:T(256)S(1)}, s32[256]{0:T(256)}, u32[]{:S(2)}) copy-start(s32[256]{0:T(256)} %param.14) | copy-start | bytes 3076
  9.4 0.7 %copy-start.8 = (s32[256]{0:T(256)S(1)}, s32[256]{0:T(256)}, u32[]{:S(2)}) copy-start(s32[256]{0:T(256)} %param.13) | copy-start | bytes 3076
  10.0 0.7 %copy-start.9 = (f32[2,2]{1,0:T(2,128)S(1)}, f32[2,2]{1,0:T(2,128)}, u32[]{:S(2)}) copy-start(f32[2,2]{1,0:T(2,128)} %vb.1) | copy-start | bytes 52

commit v2 on v1

--- a/solution.py
+++ b/solution.py
@@ -69,6 +69,21 @@
             device_id=peer, device_id_type=pl.DeviceIdType.MESH,
         )
 
+    loads = []
+    loaded = []
+    started = []
+    arrived = []
+
+    def go(*copies):
+        for copy in copies:
+            copy.start()
+            started.append(copy)
+
+    def arrive(*copies):
+        for copy in copies:
+            copy.wait_recv()
+            arrived.append(copy)
+
     barrier = pltpu.get_barrier_semaphore()
     for peer in (ypeer, ppeer, fpeer, speer, xpeer(1), xpeer(2), xpeer(3)):
         pl.semaphore_signal(barrier, inc=1, device_id=peer, device_id_type=pl.DeviceIdType.MESH)
@@ -79,7 +94,13 @@
     def local(slot, src, dst):
         copy = pltpu.make_async_copy(src, dst, lsem.at[slot])
         copy.start()
+        loads.append(copy)
         return copy
+
+    def ready(*copies):
+        for copy in copies:
+            copy.wait()
+            loaded.append(copy)
 
     ld_tok = local(0, tok, x_all.at[own_rows])
     ld_tim = local(1, tim, me_s.at[pl.ds(0, 1)])
@@ -91,18 +112,8 @@
     ld_wo = [local(9 + c, wo.at[pl.ds(c * HD, HD)], wof.at[x, yh, c]) for c in range(2)]
     ld_gu = [local(11 + c, wgu.at[c], wguv.at[:, pl.ds(c * FF, FF)]) for c in range(2)]
     ld_d = local(13, wd, wdv)
-    ld_tok.wait()
-    ld_tim.wait()
-    ld_var.wait()
-    pl.semaphore_wait(barrier, 7)
-
-    tok_y = remote(TY, x_all.at[own_rows], x_all.at[own_rows], ypeer)
-    tok_y.start()
-    tok_x = [remote(TX + k, x_all.at[own_rows], x_all.at[own_rows], xpeer(k + 1)) for k in range(3)]
-    for copy in tok_x:
-        copy.start()
-    meta = remote(ME, me_s, me_r, ppeer)
-    meta.start()
+    ready(ld_tim)
+    ready(ld_var)
 
     time_row = me_s[0:1, :].astype(F32)
     var_row = me_s[1:2, :].astype(F32)
@@ -117,7 +128,7 @@
     slot = lax.broadcasted_iota(jnp.int32, (CACHE, HW), 0)
     lane_var = lax.rem(lane, 4).astype(F32)
     in_var = (lane >= HD) & (lane < HD + 12)
-    ld_cvar.wait()
+    ready(ld_cvar)
     same = jnp.where(spread(cvr[...].astype(F32)) == lane_var, 1.0, 0.0)
     shut = jnp.where(slot >= clen[0], MASKED, 0.0)
     ke[0:CACHE, HW:] = jnp.where(lane < HD, shut, jnp.where(in_var, same, 0.0)).astype(BF16)
@@ -143,17 +154,24 @@
             dst[h, (1 - h) * HD : (2 - h) * HD, :] = jnp.zeros((HD, TOK), BF16)
 
     query_side(qe, time_row, var_row)
-    ld_v.wait()
+    ready(ld_v)
     vt[:, 0:CACHE] = vn[...].astype(F32).T.astype(BF16)
-    for copy in ld_w:
-        copy.wait()
-    for copy in ld_wo:
-        copy.wait()
-
-    tok_y.wait_send()
+    ready(ld_tok)
+    pl.semaphore_wait(barrier, 7)
+
+    tok_y = remote(TY, x_all.at[own_rows], x_all.at[own_rows], ypeer)
+    go(tok_y)
+    tok_x = [remote(TX + k, x_all.at[own_rows], x_all.at[own_rows], xpeer(k + 1)) for k in range(3)]
+    go(*tok_x)
+    meta = remote(ME, me_s, me_r, ppeer)
+    go(meta)
+
+    ready(*ld_w)
+    ready(*ld_wo)
+
+
     w1 = remote(W1, wof.at[x, yh, core], wof.at[x, yh, core], ypeer)
-    w1.start()
-
+    go(w1)
     def qkv(half):
         base = pl.multiple_of(half * HALF, HALF)
         rows = pl.ds(base, HALF)
@@ -181,23 +199,19 @@
         ke[new, 0:HW] = k.T.astype(BF16)
         vt[:, new] = v.astype(BF16)
 
-    tok_y.wait_recv()
+    arrive(tok_y)
     tok_f = [remote(TF + k, x_all.at[far_rows], x_all.at[far_rows], xpeer(k + 1)) for k in range(3)]
-    for copy in tok_f:
-        copy.start()
-    for copy in tok_x:
-        copy.wait_recv()
+    go(*tok_f)
+    arrive(*tok_x)
     keep(*qkv(yh))
     w2 = [remote(W2 + k, wof.at[x, yh, core], wof.at[x, yh, core], xpeer(k + 1)) for k in range(3)]
-    for copy in w2:
-        copy.start()
-    for copy in tok_f:
-        copy.wait_recv()
+    go(*w2)
+    arrive(*tok_f)
     rest = qkv(1 - yh)
     send_q = remote(QQ, qs, qr, ppeer)
-    send_q.start()
+    go(send_q)
     keep(*rest)
-    ld_k.wait()
+    ready(ld_k)
 
     def attend(dst, h):
         s = dot(ke[...], dst[h])
@@ -218,27 +232,24 @@
 
     both_heads(qe, qs, o1s, s1s)
     send_o1 = [remote(O1, o1s, o1r, ypeer), remote(O1 + 1, s1s, s1r, ypeer)]
-    for copy in send_o1:
-        copy.start()
-
-    meta.wait_recv()
+    go(*send_o1)
+
+    yf = 1 - yh
+    arrive(w1)
+    w3 = [remote(W3 + k, wof.at[x, yf, core], wof.at[x, yf, core], xpeer(k + 1)) for k in range(3)]
+    go(*w3)
+    w4 = [remote(W4, wof.at[x, yf, core], wof.at[x, yf, core], speer)]
+    go(w4[0])
+    arrive(meta)
     query_side(qe2, me_r[0:1, :].astype(F32), me_r[1:2, :].astype(F32))
-    send_q.wait_recv()
+    arrive(send_q)
     both_heads(qe2, qr, o2s, s2s)
     send_o2 = [
         remote(O2, o2s, o2r.at[0], ppeer), remote(O2 + 1, s2s, s2r.at[0], ppeer),
         remote(O2 + 2, o2s, o2r.at[1], fpeer), remote(O2 + 3, s2s, s2r.at[1], fpeer),
     ]
-    for copy in send_o2:
-        copy.start()
-
-    yf = 1 - yh
-    w1.wait_recv()
-    w3 = [remote(W3 + k, wof.at[x, yf, core], wof.at[x, yf, core], xpeer(k + 1)) for k in range(3)]
-    for copy in w3:
-        copy.start()
-    w4 = [remote(W4, wof.at[x, yf, core], wof.at[x, yf, core], speer)]
-    w4[0].start()
+    go(*send_o2)
+
 
     def merged(o_a, s_a, o_b, s_b):
         on = lnk[0] > 0
@@ -256,38 +267,32 @@
             )
         return jnp.concatenate(parts, axis=0).T
 
-    for copy in send_o1:
-        copy.wait_recv()
-    for copy in send_o2:
-        copy.wait_recv()
+    arrive(*send_o1)
+    arrive(*send_o2)
     mine = merged(o1s, s1s, o2r.at[0], s2r.at[0])
     other = merged(o1r, s1r, o2r.at[1], s2r.at[1])
     a3[x, :, 0:HW] = jnp.where(yh == 0, mine, other).astype(BF16)
     a3[x, :, HW:] = jnp.where(yh == 0, other, mine).astype(BF16)
     send_a = [remote(AX + k, a3.at[x], a3.at[x], xpeer(k + 1)) for k in range(3)]
-    for copy in send_a:
-        copy.start()
+    go(*send_a)
 
     for k in range(3):
-        w2[k].wait_recv()
-        w3[k].wait_recv()
+        arrive(w2[k], w3[k])
         xk = lax.rem(x + 3 - k, XN)
         copy = remote(W4 + 1 + k, wof.at[xk, :, core], wof.at[xk, :, core], speer)
-        copy.start()
+        go(copy)
         w4.append(copy)
 
-    for copy in w4:
-        copy.wait_recv()
+    arrive(*w4)
     st[...] = x_all[...].astype(F32)
     st[...] += dot(a3[x], wof[x].reshape(2 * HW, D))
     for k in (0, 2, 1):
-        send_a[k].wait_recv()
+        arrive(send_a[k])
         xk = lax.rem(x + 3 - k, XN)
         st[...] += dot(a3[xk], wof[xk].reshape(2 * HW, D))
 
-    for copy in ld_gu:
-        copy.wait()
-    ld_d.wait()
+    ready(*ld_gu)
+    ready(ld_d)
     for half in range(2):
         rows = slice(half * HALF, (half + 1) * HALF)
         stream = st[rows, :].astype(BF16).astype(F32)
@@ -304,38 +309,33 @@
 
     down(yf, far)
     send_f = [remote(RF + k, far.at[block(k + 1)], rf.at[k], xpeer(k + 1)) for k in range(3)]
-    for copy in send_f:
-        copy.start()
+    go(*send_f)
     down(yh, near)
     send_n = [remote(RN + k, near.at[block(k + 1)], rn.at[k], xpeer(k + 1)) for k in range(3)]
-    for copy in send_n:
-        copy.start()
+    go(*send_n)
     total = far[block(0), :].astype(F32)
     for k in range(3):
-        send_f[k].wait_recv()
+        arrive(send_f[k])
         total = total + rf[k].astype(F32)
     ys[...] = total.astype(BF16)
     send_y = remote(RY, ys, yr, ypeer)
-    send_y.start()
+    go(send_y)
     total = near[block(0), :].astype(F32)
     for k in range(3):
-        send_n[k].wait_recv()
+        arrive(send_n[k])
         total = total + rn[k].astype(F32)
     total = total + st[own_rows, :]
-    for copy in [tok_y][:0] + tok_x + tok_f + [meta, w1, send_q] + w2 + w3 + w4 + send_o1 + send_o2 + send_a:
+    arrive(send_y)
+    out[...] = (total + yr[...].astype(F32)).astype(BF16)
+    for copy in started:
         copy.wait_send()
-    for copy in send_f + send_n:
-        copy.wait_send()
-    send_y.wait_recv()
-    out[...] = (total + yr[...].astype(F32)).astype(BF16)
-    send_y.wait_send()
 
 
 def shards(
     tokens, variate, time_ids, cache_var, cache_len, linked, cache_kv, var_bias,
     w_qkv, w_out, w_gate_up, w_down,
 ):
-    anyspace = pl.BlockSpec(memory_space=pl.ANY)
+    anyspace = pl.BlockSpec(memory_space=pltpu.HBM)
     smem = pl.BlockSpec(memory_space=pltpu.SMEM)
     vmem = pltpu.VMEM
     scratch = [
@@ -375,7 +375,7 @@
     ]
     return pl.pallas_call(
         layer,
-        out_shape=jax.ShapeDtypeStruct((ROWS, D), BF16),
+        out_shape=pltpu.VMEM((ROWS, D), BF16),
         in_specs=[
             anyspace, anyspace, anyspace, anyspace, smem, smem, anyspace, smem,
             anyspace, anyspace, anyspace, anyspace,
@@ -383,7 +383,7 @@
         out_specs=pl.BlockSpec(memory_space=pltpu.VMEM),
         scratch_shapes=scratch,
         compiler_params=pltpu.CompilerParams(
-            collective_id=0, has_side_effects=True, vmem_limit_bytes=48 << 20
+            collective_id=0, has_side_effects=True, vmem_limit_bytes=60 << 20
         ),
         name="layer",
     )(

time: 63.1 us -> 55.2 us (0.87)
  the two profiles are of different devices: /device:TPU:12 before, /device:TPU:8 now
where the time goes in v2:
time: 55.2 us; the launch traced here: 55 us
  Pallas kernels  53.1 us (96%)
  between operations  1.3 us (2%)
  local copies, waits for them, and re-layouts  0.63 us (1%)
    pallas_call x1, Pallas kernels, shards(): pl.pallas_call(layer, out_shape=pltpu.VMEM((ROWS, D), BF16), in_specs=[an...  53.1 us

profile of v2, /device:TPU:8, one launch (start us, length us, event | category | flops | bytes accessed | tf_op | source)
XLA Modules:
  0.0 55.0 jit_solution(12570137888751040909)
XLA Ops:
  1.3 53.1 %layer.1 = bf16[32,1024]{1,0:T(8,128)(2,1)S(1)} custom-call(bf16[32,1024]{1,0:T(8,128)(2,1)} %tok.1, s32[1,256]{1,0:T(1,128)} %bitcast.4, s32[1,256]{1,0:T(1,128)} %bitcast.5, s32[1,512]{1,0:T(1,128)} %bitcast.3, s32[1]{0:T(128)S(6)} %copy.15.clen, s32[1]{0:T(128)S(6)} %copy.16.lnk, bf16[2,512,128]{2,1,0:T(8,128)(2,1)} %ckv.1, f32[2,2]{1,0:T(2,128)} %vb.1, ...), custom_call_target="tpu_custom_call" | custom-call | tf_op jit(solution)/shard_map/layer/pallas_call | solution.py:376
  54.4 0.6 %copy.14 = bf16[32,1024]{1,0:T(8,128)(2,1)} copy(bf16[32,1024]{1,0:T(8,128)(2,1)S(1)} %layer.1) | data formatting | bytes 131072

commit v3 on v2

--- a/solution.py
+++ b/solution.py
@@ -21,8 +21,11 @@
 HD = 64
 FF = 512
 
+TC = 2
+RC = 2
+
 TY, TX, TF, ME, QQ, O1, O2, AX, W1, W2, W3, W4, RF, RN, RY, NSEM = (
-    0, 1, 4, 7, 8, 9, 11, 15, 18, 19, 22, 25, 29, 32, 35, 36,
+    0, 2, 5, 11, 12, 13, 15, 19, 25, 26, 29, 32, 36, 42, 45, 47,
 )
 
 
@@ -89,7 +92,6 @@
         pl.semaphore_signal(barrier, inc=1, device_id=peer, device_id_type=pl.DeviceIdType.MESH)
 
     own_rows = pl.ds(pl.multiple_of(t * ROWS, ROWS), ROWS)
-    far_rows = pl.ds(pl.multiple_of(t_far * ROWS, ROWS), ROWS)
 
     def local(slot, src, dst):
         copy = pltpu.make_async_copy(src, dst, lsem.at[slot])
@@ -159,8 +161,12 @@
     ready(ld_tok)
     pl.semaphore_wait(barrier, 7)
 
-    tok_y = remote(TY, x_all.at[own_rows], x_all.at[own_rows], ypeer)
-    go(tok_y)
+    def piece(device, c):
+        rows = ROWS // TC
+        return x_all.at[pl.ds(pl.multiple_of(device * ROWS + c * rows, rows), rows)]
+
+    tok_y = [remote(TY + c, piece(t, c), piece(t, c), ypeer) for c in range(TC)]
+    go(*tok_y)
     tok_x = [remote(TX + k, x_all.at[own_rows], x_all.at[own_rows], xpeer(k + 1)) for k in range(3)]
     go(*tok_x)
     meta = remote(ME, me_s, me_r, ppeer)
@@ -199,9 +205,14 @@
         ke[new, 0:HW] = k.T.astype(BF16)
         vt[:, new] = v.astype(BF16)
 
-    arrive(tok_y)
-    tok_f = [remote(TF + k, x_all.at[far_rows], x_all.at[far_rows], xpeer(k + 1)) for k in range(3)]
-    go(*tok_f)
+    tok_f = []
+    for c in range(TC):
+        arrive(tok_y[c])
+        for k in range(3):
+            tok_f.append(
+                remote(TF + 3 * c + k, piece(t_far, c), piece(t_far, c), xpeer(k + 1))
+            )
+            go(tok_f[-1])
     arrive(*tok_x)
     keep(*qkv(yh))
     w2 = [remote(W2 + k, wof.at[x, yh, core], wof.at[x, yh, core], xpeer(k + 1)) for k in range(3)]
@@ -267,14 +278,21 @@
             )
         return jnp.concatenate(parts, axis=0).T
 
+    send_a = []
+
+    def share(c, upper, heads):
+        a3[x, upper] = heads.astype(BF16)
+        for k in range(3):
+            send_a.append(
+                remote(AX + 3 * c + k, a3.at[x, upper], a3.at[x, upper], xpeer(k + 1))
+            )
+            go(send_a[-1])
+
+    arrive(*send_o2[:2])
+    share(0, yh, merged(o1s, s1s, o2r.at[0], s2r.at[0]))
     arrive(*send_o1)
-    arrive(*send_o2)
-    mine = merged(o1s, s1s, o2r.at[0], s2r.at[0])
-    other = merged(o1r, s1r, o2r.at[1], s2r.at[1])
-    a3[x, :, 0:HW] = jnp.where(yh == 0, mine, other).astype(BF16)
-    a3[x, :, HW:] = jnp.where(yh == 0, other, mine).astype(BF16)
-    send_a = [remote(AX + k, a3.at[x], a3.at[x], xpeer(k + 1)) for k in range(3)]
-    go(*send_a)
+    arrive(*send_o2[2:])
+    share(1, yf, merged(o1r, s1r, o2r.at[1], s2r.at[1]))
 
     for k in range(3):
         arrive(w2[k], w3[k])
@@ -284,12 +302,16 @@
         w4.append(copy)
 
     arrive(*w4)
+    def out_part(xk):
+        heads = jnp.concatenate([a3[xk, 0], a3[xk, 1]], axis=1)
+        return dot(heads, wof[xk].reshape(2 * HW, D))
+
     st[...] = x_all[...].astype(F32)
-    st[...] += dot(a3[x], wof[x].reshape(2 * HW, D))
+    st[...] += out_part(x)
     for k in (0, 2, 1):
-        arrive(send_a[k])
+        arrive(send_a[k], send_a[3 + k])
         xk = lax.rem(x + 3 - k, XN)
-        st[...] += dot(a3[xk], wof[xk].reshape(2 * HW, D))
+        st[...] += out_part(xk)
 
     ready(*ld_gu)
     ready(ld_d)
@@ -301,32 +323,42 @@
         gate = gate_up[:, :FF]
         hid[rows, :] = (gate / (1.0 + jnp.exp(-gate)) * gate_up[:, FF:]).astype(BF16)
 
-    def down(half, dst):
-        dst[...] = dot(hid[pl.ds(pl.multiple_of(half * HALF, HALF), HALF), :], wdv[...]).astype(BF16)
+    def down(half, cols):
+        rows = pl.ds(pl.multiple_of(half * HALF, HALF), HALF)
+        return dot(hid[rows, :], wdv[:, cols]).astype(BF16)
 
     def block(k):
         return pl.ds(pl.multiple_of(lax.rem(x + k, XN) * ROWS, ROWS), ROWS)
 
-    down(yf, far)
-    send_f = [remote(RF + k, far.at[block(k + 1)], rf.at[k], xpeer(k + 1)) for k in range(3)]
-    go(*send_f)
-    down(yh, near)
+    pieces = [slice(c * (D // RC), (c + 1) * (D // RC)) for c in range(RC)]
+    send_f = []
+    for c, cols in enumerate(pieces):
+        far[c] = down(yf, cols)
+        for k in range(3):
+            send_f.append(
+                remote(RF + 3 * c + k, far.at[c, block(k + 1)], rf.at[c, k], xpeer(k + 1))
+            )
+            go(send_f[-1])
+    near[...] = down(yh, slice(0, D))
     send_n = [remote(RN + k, near.at[block(k + 1)], rn.at[k], xpeer(k + 1)) for k in range(3)]
     go(*send_n)
-    total = far[block(0), :].astype(F32)
-    for k in range(3):
-        arrive(send_f[k])
-        total = total + rf[k].astype(F32)
-    ys[...] = total.astype(BF16)
-    send_y = remote(RY, ys, yr, ypeer)
-    go(send_y)
+    send_y = []
+    for c in range(RC):
+        total = far[c, block(0), :].astype(F32)
+        for k in range(3):
+            arrive(send_f[3 * c + k])
+            total = total + rf[c, k].astype(F32)
+        ys[c] = total.astype(BF16)
+        send_y.append(remote(RY + c, ys.at[c], yr.at[c], ypeer))
+        go(send_y[c])
     total = near[block(0), :].astype(F32)
     for k in range(3):
         arrive(send_n[k])
         total = total + rn[k].astype(F32)
     total = total + st[own_rows, :]
-    arrive(send_y)
-    out[...] = (total + yr[...].astype(F32)).astype(BF16)
+    for c, cols in enumerate(pieces):
+        arrive(send_y[c])
+        out[:, cols] = (total[:, cols] + yr[c].astype(F32)).astype(BF16)
     for copy in started:
         copy.wait_send()
 
@@ -357,18 +389,18 @@
         vmem((HW, TOK), BF16), vmem((8, TOK), F32),
         vmem((HW, TOK), BF16), vmem((8, TOK), F32),
         vmem((2, HW, TOK), BF16), vmem((2, 8, TOK), F32),
-        vmem((XN, TOK, 2 * HW), BF16),
+        vmem((XN, 2, TOK, HW), BF16),
         vmem((XN, 2, 2, HD, D), BF16),
         vmem((D, 2 * FF), BF16),
         vmem((FF, D), BF16),
         vmem((TOK, D), F32),
         vmem((TOK, FF), BF16),
+        vmem((RC, HALF, D // RC), BF16),
         vmem((HALF, D), BF16),
-        vmem((HALF, D), BF16),
+        vmem((RC, 3, ROWS, D // RC), BF16),
         vmem((3, ROWS, D), BF16),
-        vmem((3, ROWS, D), BF16),
-        vmem((ROWS, D), BF16),
-        vmem((ROWS, D), BF16),
+        vmem((RC, ROWS, D // RC), BF16),
+        vmem((RC, ROWS, D // RC), BF16),
         pltpu.SemaphoreType.DMA((NSEM,)),
         pltpu.SemaphoreType.DMA((NSEM,)),
         pltpu.SemaphoreType.DMA((14,)),

time: 55.2 us -> 54 us (0.978)
  Pallas kernels: 53.1 us -> 51.9 us
    pallas_call x1, Pallas kernels: 53.1 us -> 51.9 us  [shards(): pl.pallas_call(layer, out_shape=pltpu.VMEM((ROWS, D), BF16), in_specs=[an...]
where the time goes in v3:
time: 54 us; the launch traced here: 53.8 us
  Pallas kernels  51.9 us (96%)
  between operations  1.3 us (2%)
  local copies, waits for them, and re-layouts  0.63 us (1%)
    pallas_call x1, Pallas kernels, shards(): pl.pallas_call(layer, out_shape=pltpu.VMEM((ROWS, D), BF16), in_specs=[an...  51.9 us

profile of v3, /device:TPU:8, one launch (start us, length us, event | category | flops | bytes accessed | tf_op | source)
XLA Modules:
  0.0 53.8 jit_solution(9070807264112725171)
XLA Ops:
  1.3 51.9 %layer.1 = bf16[32,1024]{1,0:T(8,128)(2,1)S(1)} custom-call(bf16[32,1024]{1,0:T(8,128)(2,1)} %tok.1, s32[1,256]{1,0:T(1,128)} %bitcast.4, s32[1,256]{1,0:T(1,128)} %bitcast.5, s32[1,512]{1,0:T(1,128)} %bitcast.3, s32[1]{0:T(128)S(6)} %copy.15.clen, s32[1]{0:T(128)S(6)} %copy.16.lnk, bf16[2,512,128]{2,1,0:T(8,128)(2,1)} %ckv.1, f32[2,2]{1,0:T(2,128)} %vb.1, ...), custom_call_target="tpu_custom_call" | custom-call | tf_op jit(solution)/shard_map/layer/pallas_call | solution.py:408
  53.2 0.6 %copy.14 = bf16[32,1024]{1,0:T(8,128)(2,1)} copy(bf16[32,1024]{1,0:T(8,128)(2,1)S(1)} %layer.1) | data formatting | bytes 131072

commit v4 on v3

--- a/solution.py
+++ b/solution.py
@@ -25,7 +25,7 @@
 RC = 2
 
 TY, TX, TF, ME, QQ, O1, O2, AX, W1, W2, W3, W4, RF, RN, RY, NSEM = (
-    0, 2, 5, 11, 12, 13, 15, 19, 25, 26, 29, 32, 36, 42, 45, 47,
+    0, 2, 5, 11, 12, 14, 17, 23, 29, 30, 33, 36, 40, 46, 49, 51,
 )
 
 
@@ -178,7 +178,9 @@
 
     w1 = remote(W1, wof.at[x, yh, core], wof.at[x, yh, core], ypeer)
     go(w1)
-    def qkv(half):
+    send_q = []
+
+    def qkv(order, half):
         base = pl.multiple_of(half * HALF, HALF)
         rows = pl.ds(base, HALF)
         normal = normed(x_all[rows, :].astype(F32)).astype(BF16)
@@ -195,7 +197,10 @@
             return jnp.concatenate(parts, axis=0)
 
         q = turned(prod[:, 0:HW].T).astype(BF16).astype(F32) * 0.125
-        qs[:, rows] = q.astype(BF16)
+        qs[half] = q.astype(BF16)
+        send = remote(QQ + order, qs.at[half], qr.at[half], ppeer)
+        go(send)
+        send_q.append(send)
         k = turned(prod[:, HW : 2 * HW].T)
         v = prod[:, 2 * HW :].T
         new = pl.ds(pl.multiple_of(base + CACHE, HALF), HALF)
@@ -214,13 +219,11 @@
             )
             go(tok_f[-1])
     arrive(*tok_x)
-    keep(*qkv(yh))
+    keep(*qkv(0, yh))
     w2 = [remote(W2 + k, wof.at[x, yh, core], wof.at[x, yh, core], xpeer(k + 1)) for k in range(3)]
     go(*w2)
     arrive(*tok_f)
-    rest = qkv(1 - yh)
-    send_q = remote(QQ, qs, qr, ppeer)
-    go(send_q)
+    rest = qkv(1, 1 - yh)
     keep(*rest)
     ready(ld_k)
 
@@ -232,18 +235,36 @@
         o = dot(vt[h * HD : (h + 1) * HD, :], p.astype(BF16))
         return o, best, total
 
-    def both_heads(dst, q, o_ref, s_ref):
+    def both_heads(dst, q, o_ref, s_ref, share_out):
         s_ref[...] = jnp.zeros(s_ref.shape, F32)
         for h in range(2):
-            dst[h, h * HD : (h + 1) * HD, :] = q[h * HD : (h + 1) * HD, :]
+            head = slice(h * HD, (h + 1) * HD)
+            for half in range(2):
+                dst[h, head, half * HALF : (half + 1) * HALF] = q[half, head, :]
             o, best, total = attend(dst, h)
-            o_ref[h * HD : (h + 1) * HD, :] = o.astype(BF16)
+            o_ref[h] = o.astype(BF16)
             s_ref[h : h + 1, :] = best
             s_ref[2 + h : 3 + h, :] = total
-
-    both_heads(qe, qs, o1s, s1s)
-    send_o1 = [remote(O1, o1s, o1r, ypeer), remote(O1 + 1, s1s, s1r, ypeer)]
-    go(*send_o1)
+            share_out(h)
+
+    send_o1 = []
+    send_o2 = [[], []]
+
+    def to_ypeer(h):
+        send_o1.append(remote(O1 + h, o1s.at[h], o1r.at[h], ypeer))
+        if h == 1:
+            send_o1.append(remote(O1 + 2, s1s, s1r, ypeer))
+        go(*send_o1[h:])
+
+    def to_partners(h):
+        for i, peer in enumerate((ppeer, fpeer)):
+            new = [remote(O2 + 3 * i + h, o2s.at[h], o2r.at[i, h], peer)]
+            if h == 1:
+                new.append(remote(O2 + 3 * i + 2, s2s, s2r.at[i], peer))
+            go(*new)
+            send_o2[i] += new
+
+    both_heads(qe, qs, o1s, s1s, to_ypeer)
 
     yf = 1 - yh
     arrive(w1)
@@ -253,20 +274,13 @@
     go(w4[0])
     arrive(meta)
     query_side(qe2, me_r[0:1, :].astype(F32), me_r[1:2, :].astype(F32))
-    arrive(send_q)
-    both_heads(qe2, qr, o2s, s2s)
-    send_o2 = [
-        remote(O2, o2s, o2r.at[0], ppeer), remote(O2 + 1, s2s, s2r.at[0], ppeer),
-        remote(O2 + 2, o2s, o2r.at[1], fpeer), remote(O2 + 3, s2s, s2r.at[1], fpeer),
-    ]
-    go(*send_o2)
-
+    arrive(*send_q)
+    both_heads(qe2, qr, o2s, s2s, to_partners)
 
     def merged(o_a, s_a, o_b, s_b):
         on = lnk[0] > 0
         parts = []
         for h in range(2):
-            head = slice(h * HD, (h + 1) * HD)
             m_a = s_a[h : h + 1, :]
             m_b = jnp.where(on, s_b[h : h + 1, :], MASKED)
             best = jnp.maximum(m_a, m_b)
@@ -274,7 +288,7 @@
             f_b = jnp.where(on, jnp.exp(m_b - best), 0.0)
             total = f_a * s_a[2 + h : 3 + h, :] + f_b * s_b[2 + h : 3 + h, :]
             parts.append(
-                (f_a * o_a[head, :].astype(F32) + f_b * o_b[head, :].astype(F32)) / total
+                (f_a * o_a[h].astype(F32) + f_b * o_b[h].astype(F32)) / total
             )
         return jnp.concatenate(parts, axis=0).T
 
@@ -288,10 +302,10 @@
             )
             go(send_a[-1])
 
-    arrive(*send_o2[:2])
+    arrive(*send_o2[0])
     share(0, yh, merged(o1s, s1s, o2r.at[0], s2r.at[0]))
     arrive(*send_o1)
-    arrive(*send_o2[2:])
+    arrive(*send_o2[1])
     share(1, yf, merged(o1r, s1r, o2r.at[1], s2r.at[1]))
 
     for k in range(3):
@@ -376,19 +390,19 @@
         vmem((KEYS, 2 * HW), BF16),
         vmem((CACHE, HW), BF16),
         vmem((HW, KEYS), BF16),
-        vmem((HW, TOK), BF16),
+        vmem((2, HW, HALF), BF16),
         vmem((2, 2 * HW, TOK), BF16),
-        vmem((HW, TOK), BF16),
+        vmem((2, HW, HALF), BF16),
         vmem((2, 2 * HW, TOK), BF16),
         vmem((2, TOK), jnp.int32),
         vmem((2, TOK), jnp.int32),
         vmem((1, CACHE), jnp.int32),
         vmem((HD // 2, TOK), F32),
         vmem((HD // 2, TOK), F32),
-        vmem((HW, TOK), BF16), vmem((8, TOK), F32),
-        vmem((HW, TOK), BF16), vmem((8, TOK), F32),
-        vmem((HW, TOK), BF16), vmem((8, TOK), F32),
-        vmem((2, HW, TOK), BF16), vmem((2, 8, TOK), F32),
+        vmem((2, HD, TOK), BF16), vmem((8, TOK), F32),
+        vmem((2, HD, TOK), BF16), vmem((8, TOK), F32),
+        vmem((2, HD, TOK), BF16), vmem((8, TOK), F32),
+        vmem((2, 2, HD, TOK), BF16), vmem((2, 8, TOK), F32),
         vmem((XN, 2, TOK, HW), BF16),
         vmem((XN, 2, 2, HD, D), BF16),
         vmem((D, 2 * FF), BF16),

time: 54 us -> 52.9 us (0.980)
  the two profiles are of different devices: /device:TPU:8 before, /device:TPU:328 now
where the time goes in v4:
time: 52.9 us; the launch traced here: 52.8 us
  Pallas kernels  50.8 us (96%)
  between operations  1.3 us (2%)
  local copies, waits for them, and re-layouts  0.63 us (1%)
    pallas_call x1, Pallas kernels, shards(): pl.pallas_call(layer, out_shape=pltpu.VMEM((ROWS, D), BF16), in_specs=[an...  50.8 us

profile of v4, /device:TPU:328, one launch (start us, length us, event | category | flops | bytes accessed | tf_op | source)
XLA Modules:
  0.0 52.8 jit_solution(3052524269214597855)
XLA Ops:
  1.3 50.8 %layer.1 = bf16[32,1024]{1,0:T(8,128)(2,1)S(1)} custom-call(bf16[32,1024]{1,0:T(8,128)(2,1)} %tok.1, s32[1,256]{1,0:T(1,128)} %bitcast.4, s32[1,256]{1,0:T(1,128)} %bitcast.5, s32[1,512]{1,0:T(1,128)} %bitcast.3, s32[1]{0:T(128)S(6)} %copy.15.clen, s32[1]{0:T(128)S(6)} %copy.16.lnk, bf16[2,512,128]{2,1,0:T(8,128)(2,1)} %ckv.1, f32[2,2]{1,0:T(2,128)} %vb.1, ...), custom_call_target="tpu_custom_call" | custom-call | tf_op jit(solution)/shard_map/layer/pallas_call | solution.py:422
  52.1 0.6 %copy.14 = bf16[32,1024]{1,0:T(8,128)(2,1)} copy(bf16[32,1024]{1,0:T(8,128)(2,1)S(1)} %layer.1) | data formatting | bytes 131072

commit v5 on v4

--- a/solution.py
+++ b/solution.py
@@ -315,31 +315,35 @@
         go(copy)
         w4.append(copy)
 
-    arrive(*w4)
-    def out_part(xk):
-        heads = jnp.concatenate([a3[xk, 0], a3[xk, 1]], axis=1)
-        return dot(heads, wof[xk].reshape(2 * HW, D))
-
-    st[...] = x_all[...].astype(F32)
-    st[...] += out_part(x)
-    for k in (0, 2, 1):
-        arrive(send_a[k], send_a[3 + k])
-        xk = lax.rem(x + 3 - k, XN)
-        st[...] += out_part(xk)
-
-    ready(*ld_gu)
-    ready(ld_d)
-    for half in range(2):
-        rows = slice(half * HALF, (half + 1) * HALF)
+    def half_rows(half):
+        return pl.ds(pl.multiple_of(half * HALF, HALF), HALF)
+
+    def out_part(rows, xk):
+        heads = jnp.concatenate([a3[xk, 0, rows, :], a3[xk, 1, rows, :]], axis=1)
+        st[rows, :] += dot(heads, wof[xk].reshape(2 * HW, D))
+
+    def feed(half, first):
+        rows = half_rows(half)
+        st[rows, :] = x_all[rows, :].astype(F32)
+        if first:
+            arrive(w4[0])
+        out_part(rows, x)
+        for k in (0, 2, 1):
+            if first:
+                arrive(w4[1 + k], send_a[k], send_a[3 + k])
+            out_part(rows, lax.rem(x + 3 - k, XN))
+        if first:
+            ready(*ld_gu)
+            ready(ld_d)
         stream = st[rows, :].astype(BF16).astype(F32)
         st[rows, :] = stream
         gate_up = dot(normed(stream).astype(BF16), wguv[...])
         gate = gate_up[:, :FF]
         hid[rows, :] = (gate / (1.0 + jnp.exp(-gate)) * gate_up[:, FF:]).astype(BF16)
 
+    feed(yf, True)
     def down(half, cols):
-        rows = pl.ds(pl.multiple_of(half * HALF, HALF), HALF)
-        return dot(hid[rows, :], wdv[:, cols]).astype(BF16)
+        return dot(hid[half_rows(half), :], wdv[:, cols]).astype(BF16)
 
     def block(k):
         return pl.ds(pl.multiple_of(lax.rem(x + k, XN) * ROWS, ROWS), ROWS)
@@ -353,6 +357,7 @@
                 remote(RF + 3 * c + k, far.at[c, block(k + 1)], rf.at[c, k], xpeer(k + 1))
             )
             go(send_f[-1])
+    feed(yh, False)
     near[...] = down(yh, slice(0, D))
     send_n = [remote(RN + k, near.at[block(k + 1)], rn.at[k], xpeer(k + 1)) for k in range(3)]
     go(*send_n)

time: 52.9 us -> 52.5 us (level)
  the two profiles are of different devices: /device:TPU:328 before, /device:TPU:200 now
where the time goes in v5:
time: 52.5 us; the launch traced here: 52.4 us
  Pallas kernels  50.4 us (96%)
  between operations  1.3 us (2%)
  local copies, waits for them, and re-layouts  0.63 us (1%)
    pallas_call x1, Pallas kernels, shards(): pl.pallas_call(layer, out_shape=pltpu.VMEM((ROWS, D), BF16), in_specs=[an...  50.4 us

profile of v5, /device:TPU:200, one launch (start us, length us, event | category | flops | bytes accessed | tf_op | source)
XLA Modules:
  0.0 52.4 jit_solution(666465694422351421)
XLA Ops:
  1.3 50.4 %layer.1 = bf16[32,1024]{1,0:T(8,128)(2,1)S(1)} custom-call(bf16[32,1024]{1,0:T(8,128)(2,1)} %tok.1, s32[1,256]{1,0:T(1,128)} %bitcast.4, s32[1,256]{1,0:T(1,128)} %bitcast.5, s32[1,512]{1,0:T(1,128)} %bitcast.3, s32[1]{0:T(128)S(6)} %copy.15.clen, s32[1]{0:T(128)S(6)} %copy.16.lnk, bf16[2,512,128]{2,1,0:T(8,128)(2,1)} %ckv.1, f32[2,2]{1,0:T(2,128)} %vb.1, ...), custom_call_target="tpu_custom_call" | custom-call | tf_op jit(solution)/shard_map/layer/pallas_call | solution.py:427
  51.7 0.6 %copy.14 = bf16[32,1024]{1,0:T(8,128)(2,1)} copy(bf16[32,1024]{1,0:T(8,128)(2,1)S(1)} %layer.1) | data formatting | bytes 131072

commit v6 on v5

--- a/solution.py
+++ b/solution.py
@@ -257,12 +257,16 @@
         go(*send_o1[h:])
 
     def to_partners(h):
-        for i, peer in enumerate((ppeer, fpeer)):
-            new = [remote(O2 + 3 * i + h, o2s.at[h], o2r.at[i, h], peer)]
-            if h == 1:
-                new.append(remote(O2 + 3 * i + 2, s2s, s2r.at[i], peer))
+        new = [remote(O2 + h, o2s.at[h], o2r.at[0, h], ppeer)]
+        if h == 1:
+            new.append(remote(O2 + 2, s2s, s2r.at[0], ppeer))
+        go(*new)
+        send_o2[0].extend(new)
+        if h == 1:
+            new = [remote(O2 + 3 + i, o2s.at[i], o2r.at[1, i], fpeer) for i in range(2)]
+            new.append(remote(O2 + 5, s2s, s2r.at[1], fpeer))
             go(*new)
-            send_o2[i] += new
+            send_o2[1].extend(new)
 
     both_heads(qe, qs, o1s, s1s, to_ypeer)
 

time: 52.5 us -> 52.9 us (level)
  the two profiles are of different devices: /device:TPU:200 before, /device:TPU:456 now
where the time goes in v6:
time: 52.9 us; the launch traced here: 52.7 us
  Pallas kernels  50.8 us (96%)
  between operations  1.3 us (2%)
  local copies, waits for them, and re-layouts  0.63 us (1%)
    pallas_call x1, Pallas kernels, shards(): pl.pallas_call(layer, out_shape=pltpu.VMEM((ROWS, D), BF16), in_specs=[an...  50.8 us

profile of v6, /device:TPU:456, one launch (start us, length us, event | category | flops | bytes accessed | tf_op | source)
XLA Modules:
  0.0 52.7 jit_solution(12984593078322744407)
XLA Ops:
  1.3 50.8 %layer.1 = bf16[32,1024]{1,0:T(8,128)(2,1)S(1)} custom-call(bf16[32,1024]{1,0:T(8,128)(2,1)} %tok.1, s32[1,256]{1,0:T(1,128)} %bitcast.4, s32[1,256]{1,0:T(1,128)} %bitcast.5, s32[1,512]{1,0:T(1,128)} %bitcast.3, s32[1]{0:T(128)S(6)} %copy.15.clen, s32[1]{0:T(128)S(6)} %copy.16.lnk, bf16[2,512,128]{2,1,0:T(8,128)(2,1)} %ckv.1, f32[2,2]{1,0:T(2,128)} %vb.1, ...), custom_call_target="tpu_custom_call" | custom-call | tf_op jit(solution)/shard_map/layer/pallas_call | solution.py:431
  52.1 0.6 %copy.14 = bf16[32,1024]{1,0:T(8,128)(2,1)} copy(bf16[32,1024]{1,0:T(8,128)(2,1)S(1)} %layer.1) | data formatting | bytes 131072
